TPU v7x, 32 devices: a whole 2x2x4 slice. The times are simulated.
32 devices in a mesh: dp: 8 (over z, x), mp: 4 (over y, core).
Axes of the slice: x: 2, y: 2, z: 4, core: 2. Of those that a mesh axis runs over, the one named last changes fastest.
Arguments:
- activations: bfloat16 [4096, 3072], P('dp', 'mp'), may hold values from -6 to 6
- out_grads: bfloat16 [4096, 6144], P('dp', 'mp'), may hold values from -0.25 to 0.25
- error: bfloat16 [8, 3072, 6144], P('dp', 'mp'), may hold values from -8 to 8
- sketch: bfloat16 [6144, 64], replicated, may hold values from -0.078125 to 0.078125
- momentum: float32 [3072, 6144], P('mp', 'dp'), may hold values from -6 to 6
Outputs:
- error_new: bfloat16 [8, 3072, 6144], P('dp', 'mp')
- momentum_new: float32 [3072, 6144], P('mp', 'dp')
- next_sketch: bfloat16 [6144, 64], replicated
All inputs are finite; a program needn't handle non-finite values.
Results may differ from a plain program's by a relative error of at most 0.0057.
Values may be sent and summed in bfloat16 or wider, within the bound.
A program may use at most 64 MiB of HBM per device.

v0:
```python
import jax
import jax.numpy as jnp
from jax import lax
from jax.sharding import PartitionSpec as P

beta_decay = 0.9


def update_momentum(momentum, basis_rows, sketch_block):
    product = lax.dot_general(
        basis_rows, sketch_block, (((1,), (1,)), ((), ())), preferred_element_type=jnp.float32
    )
    return beta_decay * momentum + product


def local(activations, out_grads, error, sketch, momentum):
    own_error = error[0]
    product = lax.dot_general(
        activations,
        lax.all_gather(out_grads, "mp", axis=1, tiled=True),
        (((0,), (0,)), ((), ())),
        preferred_element_type=jnp.float32,
    )
    accumulated = (product + own_error.astype(jnp.float32)).astype(jnp.bfloat16)
    local_left = jnp.dot(accumulated, sketch, preferred_element_type=jnp.float32)
    left_sketch = lax.psum(local_left, "dp")
    gram_local = jnp.dot(
        left_sketch.T,
        left_sketch,
        precision=lax.Precision.HIGHEST,
        preferred_element_type=jnp.float32,
    )
    gram_matrix = lax.psum(gram_local, "mp")
    factor = jnp.linalg.cholesky(gram_matrix)
    basis_rows = jax.scipy.linalg.solve_triangular(factor, left_sketch.T, lower=True).T.astype(
        jnp.bfloat16
    )
    block_width = momentum.shape[1]
    local_right = lax.dot_general(
        accumulated, basis_rows, (((0,), (0,)), ((), ())), preferred_element_type=jnp.float32
    )
    right_sketch = lax.psum(local_right, ("dp", "mp"))
    next_sketch = right_sketch.astype(jnp.bfloat16)
    sketch_part = lax.dynamic_slice_in_dim(
        next_sketch, lax.axis_index("dp") * block_width, block_width, 0
    )
    momentum_new = update_momentum(momentum, basis_rows, sketch_part)
    decoded = lax.dot_general(
        basis_rows, next_sketch, (((1,), (1,)), ((), ())), preferred_element_type=jnp.float32
    )
    error_new = (accumulated.astype(jnp.float32) - decoded / lax.axis_size("dp")).astype(
        jnp.bfloat16
    )
    return (error_new[None], momentum_new, next_sketch)


def solution(mesh):
    in_specs = (P("dp", "mp"), P("dp", "mp"), P("dp", "mp", None), P(), P("mp", "dp"))
    out_specs = (P("dp", "mp", None), P("mp", "dp"), P())
    return jax.shard_map(local, mesh=mesh, in_specs=in_specs, out_specs=out_specs, check_vma=False)
```

profile of v0, /device:TPU:0, one launch (start us, length us, event | category | flops | bytes accessed | tf_op | source)
XLA Modules:
  0.0 249.4 jit_solution(14047941913646381180)
XLA Ops:
  7.2 0.0 copy-start
  7.2 0.0 all-gather.2.cloned.1.call-start
  7.2 0.7 all-gather.2.cloned.1.call-update
  7.9 0.0 copy-start.4
  7.9 0.0 all-reduce.3.cloned.1.call-start
  8.0 50.7 %all-gather.2.cloned.1.call-done = bf16[512,6144]{1,0:T(8,128)(2,1)} async-done(((bf16[512,1536]{1,0:T(8,128)(2,1)}), bf16[512,6144]{1,0:T(8,128)(2,1)}) %all-gather.2.cloned.1.call-update) | async-done | bytes 6291472 | tf_op jit(solution)/shard_map/all_gather | solution.py:20
  58.7 0.0 copy-done
  58.7 9.6 %fusion = bf16[768,6144]{1,0:T(8,128)(2,1)S(1)} fusion(bf16[1,768,6144]{2,1,0:T(8,128)(2,1)} %param.7, bf16[512,768]{1,0:T(8,128)(2,1)S(1)} %copy-done, bf16[512,6144]{1,0:T(8,128)(2,1)} %all-gather.2.cloned.1.call-done), kind=kOutput, calls=%fused_computation.1 | convolution fusion | flops 4845993984 | bytes 25952256 | tf_op jit(solution)/shard_map/dot_general | solution.py:18
  68.3 0.0 copy-start.1
  68.3 3.7 %copy-done.1 = bf16[768,6144]{1,0:T(8,128)(2,1)} copy-done((bf16[768,6144]{1,0:T(8,128)(2,1)}, bf16[768,6144]{1,0:T(8,128)(2,1)S(1)}, u32[]{:S(2)}) %copy-start.1) | copy-done | bytes 9437208
  72.1 0.0 copy-done.4
  72.1 3.7 %fusion.7 = f32[768,64]{0,1:T(8,128)} fusion(bf16[768,6144]{1,0:T(8,128)(2,1)S(1)} %fusion, bf16[6144,64]{0,1:T(8,128)(2,1)S(1)} %copy-done.4), kind=kOutput, calls=%fused_computation.17 | convolution fusion | flops 603979776 | bytes 10420224 | tf_op jit(solution)/shard_map/dot_general | solution.py:25
  75.7 0.0 all-reduce.3.cloned.1.call-update
  75.8 70.8 %all-reduce.3.cloned.1.call-done = f32[768,64]{0,1:T(8,128)} async-done(((f32[768,64]{0,1:T(8,128)}), f32[768,64]{0,1:T(8,128)}) %all-reduce.3.cloned.1.call-update) | async-done | bytes 196624 | tf_op jit(solution)/shard_map/psum | solution.py:26
  146.6 1.3 fusion.8
  147.9 10.3 %psum.22 = f32[64,64]{0,1:T(8,128)S(1)} all-reduce(f32[64,64]{0,1:T(8,128)S(1)} %fusion.8), channel_id=1, replica_groups=mesh['dp'=8,'mp'=4] {'mp'}, use_global_device_ids=true, to_apply=%region_1.0 | all-reduce | flops 4096 | bytes 32768 | tf_op jit(solution)/shard_map/psum | solution.py:33
  158.2 0.1 copy.9
  158.3 5.8 %cholesky.16 = f32[64,64]{1,0:T(8,128)S(1)} custom-call(f32[64,64]{1,0:T(8,128)S(1)} %fusion.5), custom_call_target="Cholesky" | custom-call | tf_op jit(solution)/shard_map/jit(cholesky)/cholesky | solution.py:34
  164.2 0.6 compare_reduce_fusion
  164.8 0.7 fusion.3
  165.5 4.9 %custom-call.7 = f32[1,64,64]{1,2,0:T(8,128)S(1)} custom-call(f32[1,64,64]{2,1,0:T(8,128)S(1)} %fusion.3), custom_call_target="InvertDiagBlocksLowerTriangular" | custom-call | tf_op jit(solution)/shard_map/jit(_solve_triangular)/triangular_solve | solution.py:35
  170.4 1.3 convolution_convert_fusion
  171.7 5.4 %fusion.9 = f32[6144,64]{0,1:T(8,128)S(1)} fusion(bf16[768,64]{0,1:T(8,128)(2,1)S(1)} %convolution_convert_fusion, bf16[768,6144]{1,0:T(8,128)(2,1)} %copy-done.1), kind=kOutput, calls=%fused_computation.19 | convolution fusion | flops 603979776 | bytes 11108352 | tf_op jit(solution)/shard_map/dot_general | solution.py:39
  177.1 55.7 %all-reduce.4 = bf16[6144,64]{0,1:T(8,128)(2,1)S(1)} all-reduce(f32[6144,64]{0,1:T(8,128)S(1)} %fusion.9), channel_id=1, replica_groups=mesh['dp'=8,'mp'=4] {'dp','mp'}, use_global_device_ids=true, to_apply=%region_4.5 | all-reduce | flops 393216 | bytes 2359296 | tf_op jit(solution)/shard_map/psum | solution.py:42
  232.8 0.0 copy-start.2
  232.8 0.0 copy-start.3
  232.8 7.8 %fusion.1 = bf16[1,768,6144]{2,1,0:T(8,128)(2,1)} fusion(bf16[768,64]{0,1:T(8,128)(2,1)S(1)} %convolution_convert_fusion, bf16[6144,64]{0,1:T(8,128)(2,1)S(1)} %all-reduce.4, bf16[768,6144]{1,0:T(8,128)(2,1)} %copy-done.1), kind=kOutput, calls=%fused_computation.3 | convolution fusion | flops 622854144 | bytes 19759104 | tf_op jit(solution)/shard_map/dot_general | solution.py:48
  240.7 0.0 copy-done.2
  240.7 0.0 copy-done.3
  240.7 1.9 multiply_add_fusion
  (2 shorter events, 0.0 us)
Async XLA Ops:
  7.2 51.5 %copy-start = (bf16[512,768]{1,0:T(8,128)(2,1)S(1)}, bf16[512,768]{1,0:T(8,128)(2,1)}, u32[]{:S(2)}) copy-start(bf16[512,768]{1,0:T(8,128)(2,1)} %param.5) | copy-start | bytes 2359300
  7.2 51.5 %all-gather.2.cloned.1.call-start = ((), (), s32[]{:S(2)}) async-start(), calls=%async_computation | async-start | bytes 7864320 | tf_op jit(solution)/shard_map/all_gather | solution.py:20
  7.9 64.2 %copy-start.4 = (bf16[6144,64]{0,1:T(8,128)(2,1)S(1)}, bf16[6144,64]{0,1:T(8,128)(2,1)}, u32[]{:S(2)}) copy-start(bf16[6144,64]{0,1:T(8,128)(2,1)} %param.8) | copy-start | bytes 2359300
  7.9 138.7 %all-reduce.3.cloned.1.call-start = ((), (), s32[]{:S(2)}) async-start(), calls=%async_computation.1 | async-start | bytes 393216 | tf_op jit(solution)/shard_map/psum | solution.py:26
  68.3 3.7 %copy-start.1 = (bf16[768,6144]{1,0:T(8,128)(2,1)}, bf16[768,6144]{1,0:T(8,128)(2,1)S(1)}, u32[]{:S(2)}) copy-start(bf16[768,6144]{1,0:T(8,128)(2,1)S(1)} %fusion) | copy-start | bytes 28311556
  232.8 7.8 %copy-start.2 = (bf16[6144,64]{0,1:T(8,128)(2,1)}, bf16[6144,64]{0,1:T(8,128)(2,1)S(1)}, u32[]{:S(2)}) copy-start(bf16[6144,64]{0,1:T(8,128)(2,1)S(1)} %all-reduce.4) | copy-start | bytes 2359300
  232.8 7.8 %copy-start.3 = (f32[768,768]{1,0:T(8,128)S(1)}, f32[768,768]{1,0:T(8,128)}, u32[]{:S(2)}) copy-start(f32[768,768]{1,0:T(8,128)} %param.9) | copy-start | bytes 7077892
Sparse Core Ops, SparseCore 0:
  9.5 49.0 all-gather.1
  75.9 70.6 all-reduce.2
where the time goes:
time: 250 us; the launch traced here: 249 us
  waiting for transfers between devices  122 us (49%)
  blocking collectives  66 us (26%)
  matrix products  31.1 us (12%)
  between operations  14.2 us (6%)
  other arithmetic  12.1 us (5%)
  local copies, waits for them, and re-layouts  3.84 us (2%)
    psum x1, waiting for transfers between devices, local(): left_sketch = lax.psum(local_left, 'dp')  70.8 us
    psum x1, blocking collectives, local(): right_sketch = lax.psum(local_right, ('dp', 'mp'))  55.7 us
    all_gather x1, waiting for transfers between devices, local(): lax.all_gather(out_grads, 'mp', axis=1, tiled=True)  50.7 us
    psum x1, blocking collectives, local(): gram_matrix = lax.psum(gram_local, 'mp')  10.3 us
    dot_general x1, matrix products, local(): lax.dot_general(activations, lax.all_gather(out_grads, 'mp', axis=1, tile...  9.64 us
    dot_general x1, matrix products, local(): lax.dot_general(basis_rows, next_sketch, (((1,), (1,)), ((), ())), prefer...  7.81 us
    another operation x3, other arithmetic, local(): factor = jnp.linalg.cholesky(gram_matrix)  6.52 us
    another operation x2, other arithmetic, local(): jax.scipy.linalg.solve_triangular(factor, left_sketch.T, lower=True)  5.55 us
  transfers between devices with their start and end apart: 2, of which 2 were waited for; matrix products, arithmetic and copies ran while one was open for 0% of the time, Pallas kernels for 0%

commit v1 on v0

--- a/solution.py
+++ b/solution.py
@@ -39,7 +39,9 @@
     local_right = lax.dot_general(
         accumulated, basis_rows, (((0,), (0,)), ((), ())), preferred_element_type=jnp.float32
     )
-    right_sketch = lax.psum(local_right, ("dp", "mp"))
+    right_sketch = local_right
+    for mesh_axis in ("mp", "dp"):
+        right_sketch = lax.psum(right_sketch, mesh_axis)
     next_sketch = right_sketch.astype(jnp.bfloat16)
     sketch_part = lax.dynamic_slice_in_dim(
         next_sketch, lax.axis_index("dp") * block_width, block_width, 0

time: 250 us -> 318 us (1.27)
  waiting for transfers between devices: 122 us -> 164 us
  blocking collectives: 66 us -> 91.3 us
    psum x0 -> x1, waiting for transfers between devices: none -> 42.2 us  [local(): right_sketch = lax.psum(right_sketch, mesh_axis)]
    psum x1, blocking collectives: 55.7 us -> 81 us  [local(): right_sketch = lax.psum(right_sketch, mesh_axis)]
  transfers between devices with their start and end apart: 2 -> 3, of which waited for: 2 -> 3; matrix products, arithmetic and copies ran while one was open for 0% -> 0% of each run, Pallas kernels for 0% -> 0%
where the time goes in v1:
time: 318 us
  waiting for transfers between devices  164 us (52%)
  blocking collectives  91.3 us (29%)
  matrix products  32.2 us (10%)
  between operations  13.9 us (4%)
  other arithmetic  12.1 us (4%)
  local copies, waits for them, and re-layouts  3.84 us (1%)
    psum x1, blocking collectives, local(): right_sketch = lax.psum(right_sketch, mesh_axis)  81 us
    psum x1, waiting for transfers between devices, local(): left_sketch = lax.psum(local_left, 'dp')  70.8 us
    all_gather x1, waiting for transfers between devices, local(): lax.all_gather(out_grads, 'mp', axis=1, tiled=True)  50.7 us
    psum x1, waiting for transfers between devices, local(): right_sketch = lax.psum(right_sketch, mesh_axis)  42.2 us
    psum x1, blocking collectives, local(): gram_matrix = lax.psum(gram_local, 'mp')  10.3 us
    dot_general x1, matrix products, local(): lax.dot_general(activations, lax.all_gather(out_grads, 'mp', axis=1, tile...  9.64 us
    dot_general x1, matrix products, local(): lax.dot_general(basis_rows, next_sketch, (((1,), (1,)), ((), ())), prefer...  7.81 us
    dot_general x1, matrix products, local(): lax.dot_general(accumulated, basis_rows, (((0,), (0,)), ((), ())), prefer...  6.58 us
  transfers between devices with their start and end apart: 3, of which 3 were waited for; matrix products, arithmetic and copies ran while one was open for 0% of the time, Pallas kernels for 0%

profile of v1, /device:TPU:0, one launch (start us, length us, event | category | flops | bytes accessed | tf_op | source)
XLA Modules:
  0.0 317.8 jit_solution(17936509633370515472)
XLA Ops:
  7.2 0.0 copy-start
  7.2 0.0 all-gather.2.cloned.1.call-start
  7.2 0.7 all-gather.2.cloned.1.call-update
  7.9 0.0 copy-start.4
  7.9 0.0 all-reduce.4.cloned.1.call-start
  8.0 50.7 %all-gather.2.cloned.1.call-done = bf16[512,6144]{1,0:T(8,128)(2,1)} async-done(((bf16[512,1536]{1,0:T(8,128)(2,1)}), bf16[512,6144]{1,0:T(8,128)(2,1)}) %all-gather.2.cloned.1.call-update) | async-done | bytes 6291472 | tf_op jit(solution)/shard_map/all_gather | solution.py:20
  58.7 0.0 copy-done
  58.7 9.6 %fusion = bf16[768,6144]{1,0:T(8,128)(2,1)S(1)} fusion(bf16[1,768,6144]{2,1,0:T(8,128)(2,1)} %param.7, bf16[512,768]{1,0:T(8,128)(2,1)S(1)} %copy-done, bf16[512,6144]{1,0:T(8,128)(2,1)} %all-gather.2.cloned.1.call-done), kind=kOutput, calls=%fused_computation.1 | convolution fusion | flops 4845993984 | bytes 25952256 | tf_op jit(solution)/shard_map/dot_general | solution.py:18
  68.3 0.0 copy-start.1
  68.3 3.7 %copy-done.1 = bf16[768,6144]{1,0:T(8,128)(2,1)} copy-done((bf16[768,6144]{1,0:T(8,128)(2,1)}, bf16[768,6144]{1,0:T(8,128)(2,1)S(1)}, u32[]{:S(2)}) %copy-start.1) | copy-done | bytes 9437208
  72.1 0.0 copy-done.4
  72.1 3.7 %fusion.7 = f32[768,64]{0,1:T(8,128)} fusion(bf16[768,6144]{1,0:T(8,128)(2,1)S(1)} %fusion, bf16[6144,64]{0,1:T(8,128)(2,1)S(1)} %copy-done.4), kind=kOutput, calls=%fused_computation.17 | convolution fusion | flops 603979776 | bytes 10420224 | tf_op jit(solution)/shard_map/dot_general | solution.py:25
  75.7 0.0 all-reduce.4.cloned.1.call-update
  75.7 0.0 all-reduce.6.cloned.1.call-start
  75.8 70.8 %all-reduce.4.cloned.1.call-done = f32[768,64]{0,1:T(8,128)} async-done(((f32[768,64]{0,1:T(8,128)}), f32[768,64]{0,1:T(8,128)}) %all-reduce.4.cloned.1.call-update) | async-done | bytes 196624 | tf_op jit(solution)/shard_map/psum | solution.py:26
  146.6 1.3 fusion.8
  147.9 10.3 %psum.29 = f32[64,64]{0,1:T(8,128)S(1)} all-reduce(f32[64,64]{0,1:T(8,128)S(1)} %fusion.8), channel_id=1, replica_groups=mesh['dp'=8,'mp'=4] {'mp'}, use_global_device_ids=true, to_apply=%region_1.0 | all-reduce | flops 4096 | bytes 32768 | tf_op jit(solution)/shard_map/psum | solution.py:33
  158.2 0.1 copy.9
  158.3 5.8 %cholesky.16 = f32[64,64]{1,0:T(8,128)S(1)} custom-call(f32[64,64]{1,0:T(8,128)S(1)} %fusion.5), custom_call_target="Cholesky" | custom-call | tf_op jit(solution)/shard_map/jit(cholesky)/cholesky | solution.py:34
  164.2 0.6 compare_reduce_fusion
  164.8 0.7 fusion.3
  165.5 4.9 %custom-call.7 = f32[1,64,64]{1,2,0:T(8,128)S(1)} custom-call(f32[1,64,64]{2,1,0:T(8,128)S(1)} %fusion.3), custom_call_target="InvertDiagBlocksLowerTriangular" | custom-call | tf_op jit(solution)/shard_map/jit(_solve_triangular)/triangular_solve | solution.py:35
  170.4 1.3 convolution_convert_fusion
  171.7 6.6 %fusion.9 = f32[6144,64]{0,1:T(8,128)} fusion(bf16[768,64]{0,1:T(8,128)(2,1)S(1)} %convolution_convert_fusion, bf16[768,6144]{1,0:T(8,128)(2,1)} %copy-done.1), kind=kOutput, calls=%fused_computation.19 | convolution fusion | flops 603979776 | bytes 11108352 | tf_op jit(solution)/shard_map/dot_general | solution.py:39
  178.3 0.0 all-reduce.6.cloned.1.call-update
  178.3 42.2 %all-reduce.6.cloned.1.call-done = f32[6144,64]{0,1:T(8,128)} async-done(((f32[6144,64]{0,1:T(8,128)}), f32[6144,64]{0,1:T(8,128)}) %all-reduce.6.cloned.1.call-update) | async-done | bytes 1572880 | tf_op jit(solution)/shard_map/psum | solution.py:44
  220.5 81.0 %all-reduce.7 = bf16[6144,64]{0,1:T(8,128)(2,1)S(1)} all-reduce(f32[6144,64]{0,1:T(8,128)} %all-reduce.6.cloned.1.call-done), channel_id=1, replica_groups=mesh['dp'=8,'mp'=4] {'dp'}, use_global_device_ids=true, to_apply=%region_5.6 | all-reduce | flops 393216 | bytes 2359296 | tf_op jit(solution)/shard_map/psum | solution.py:44
  301.5 0.0 copy-start.2
  301.5 0.0 copy-start.3
  301.5 7.8 %fusion.1 = bf16[1,768,6144]{2,1,0:T(8,128)(2,1)} fusion(bf16[768,64]{0,1:T(8,128)(2,1)S(1)} %convolution_convert_fusion, bf16[6144,64]{0,1:T(8,128)(2,1)S(1)} %all-reduce.7, bf16[768,6144]{1,0:T(8,128)(2,1)} %copy-done.1), kind=kOutput, calls=%fused_computation.3 | convolution fusion | flops 622854144 | bytes 19759104 | tf_op jit(solution)/shard_map/dot_general | solution.py:50
  309.3 0.0 copy-done.2
  309.3 1.9 multiply_add_fusion
  (3 shorter events, 0.0 us)
Async XLA Ops:
  7.2 51.5 %copy-start = (bf16[512,768]{1,0:T(8,128)(2,1)S(1)}, bf16[512,768]{1,0:T(8,128)(2,1)}, u32[]{:S(2)}) copy-start(bf16[512,768]{1,0:T(8,128)(2,1)} %param.5) | copy-start | bytes 2359300
  7.2 51.5 %all-gather.2.cloned.1.call-start = ((), (), s32[]{:S(2)}) async-start(), calls=%async_computation | async-start | bytes 7864320 | tf_op jit(solution)/shard_map/all_gather | solution.py:20
  7.9 64.2 %copy-start.4 = (bf16[6144,64]{0,1:T(8,128)(2,1)S(1)}, bf16[6144,64]{0,1:T(8,128)(2,1)}, u32[]{:S(2)}) copy-start(bf16[6144,64]{0,1:T(8,128)(2,1)} %param.8) | copy-start | bytes 2359300
  7.9 138.7 %all-reduce.4.cloned.1.call-start = ((), (), s32[]{:S(2)}) async-start(), calls=%async_computation.1 | async-start | bytes 393216 | tf_op jit(solution)/shard_map/psum | solution.py:26
  68.3 3.7 %copy-start.1 = (bf16[768,6144]{1,0:T(8,128)(2,1)}, bf16[768,6144]{1,0:T(8,128)(2,1)S(1)}, u32[]{:S(2)}) copy-start(bf16[768,6144]{1,0:T(8,128)(2,1)S(1)} %fusion) | copy-start | bytes 28311556
  75.7 144.7 %all-reduce.6.cloned.1.call-start = ((), (), s32[]{:S(2)}) async-start(), calls=%async_computation.2 | async-start | bytes 3145728 | tf_op jit(solution)/shard_map/psum | solution.py:44
  301.5 7.8 %copy-start.2 = (bf16[6144,64]{0,1:T(8,128)(2,1)}, bf16[6144,64]{0,1:T(8,128)(2,1)S(1)}, u32[]{:S(2)}) copy-start(bf16[6144,64]{0,1:T(8,128)(2,1)S(1)} %all-reduce.7) | copy-start | bytes 2359300
  301.5 7.8 %copy-start.3 = (f32[768,768]{1,0:T(8,128)S(1)}, f32[768,768]{1,0:T(8,128)}, u32[]{:S(2)}) copy-start(f32[768,768]{1,0:T(8,128)} %param.9) | copy-start | bytes 7077892
Sparse Core Ops, SparseCore 0:
  9.5 49.0 all-gather.1
  75.9 70.6 all-reduce.3
  178.4 42.0 all-reduce.5
